TPU v7x, 32 devices: a whole 2x2x4 slice. The times are simulated.
32 devices in a mesh: sub: 8 (over y, x, core), front: 4 (over z).
Axes of the slice: x: 2, y: 2, z: 4, core: 2. Of those that a mesh axis runs over, the one named last changes fastest.
Arguments:
- front_inverse: bfloat16 [8, 8192, 2048], P('sub', 'front'), may hold values from -0.75 to 0.75
- coupling: bfloat16 [8, 8192, 2048], P('sub', 'front'), may hold values from -0.0234375 to 0.0234375
- free_modes: bfloat16 [8, 300, 8192], P('sub', None, 'front'), may hold values from -0.125 to 0.125
- dof_offset: int32 [8, 256], P('sub', 'front'), may hold values from 0 to 2047, as said below
- interface_id: int32 [8, 256], replicated, may hold values from 0 to 1023, as said below
Outputs:
- attachment: bfloat16 [8, 256, 8192], P('sub', None, 'front')
- flexibility: float32 [1024, 1024], P(('sub', 'front'))
Inputs may be any that keep to these rules, and one draw needn't show every extreme that they name: `dof_offset`: within one substructure and one front the 64 offsets are distinct, and 0 and 2047 occur among them. `interface_id`: every value occurs exactly twice in the whole array.
All inputs are finite; a program needn't handle non-finite values.
Results may differ from a plain program's by a relative error of at most 0.02.
Values may be sent and summed in bfloat16 or wider, within the bound.
No kernel may reach another device: no remote copies, remote signals or barrier semaphores. Data moves between devices by JAX's collectives and lax.ppermute only.
A program may use at most 128 MiB of HBM per device.

v0:
```python
import jax
import jax.numpy as jnp
from jax import lax
from jax.sharding import PartitionSpec as P


def shifted(value, axis, steps):
    count = lax.axis_size(axis)
    leading, last = (max(0, -steps), min(count, count - steps))
    return lax.ppermute(value, axis, [(source, source + steps) for source in range(leading, last)])


def contract_last(left, right):
    return lax.dot_general(
        left, right, (((1,), (1,)), ((), ())), preferred_element_type=jnp.float32
    )


def on_device(front_inverse, coupling, free_modes, dof_offset, interface_id):
    inverse_block = front_inverse[0]
    coupling_block = coupling[0]
    mode_block = free_modes[0]
    offsets = dof_offset[0]
    order = inverse_block.shape[0]
    columns_all = interface_id.shape[1]
    per_front = offsets.shape[0]
    fronts = lax.axis_size("front")
    front_pos = lax.axis_index("front")
    sub_pos = lax.axis_index("sub")
    column_ids = jnp.arange(columns_all, dtype=jnp.int32)
    local_ids = jnp.arange(per_front, dtype=jnp.int32)
    row_ids = jnp.arange(order, dtype=jnp.int32)
    column_pick = (column_ids[:, None] == front_pos * per_front + local_ids[None, :]).astype(
        jnp.float32
    )
    row_pick = (offsets[:, None] == row_ids[None, :]).astype(jnp.float32)
    forces = jnp.dot(column_pick, row_pick, precision=lax.Precision.HIGHEST)
    groups = 1
    width = columns_all // groups
    force_groups = forces.reshape(groups, width, order)
    moments = groups + fronts - 1

    def forward(moment, carry):
        solved, outgoing = carry
        incoming = shifted(outgoing, "front", 1)
        panel = moment - front_pos
        valid = (panel >= 0) & (panel < groups)
        clipped = jnp.clip(panel, 0, groups - 1)

        def forward_active(unused):
            load = lax.dynamic_index_in_dim(force_groups, clipped, 0, keepdims=False)
            reduced = (load - contract_last(incoming, coupling_block)).astype(jnp.bfloat16)
            return contract_last(reduced, inverse_block).astype(jnp.bfloat16)

        def forward_waiting(unused):
            return outgoing

        result = lax.cond(valid, forward_active, forward_waiting, 0)
        solved = lax.dynamic_update_index_in_dim(solved, result, clipped, 0)
        return (solved, result)

    forward_start = (
        jnp.zeros((groups, width, order), jnp.bfloat16),
        jnp.zeros((width, order), jnp.bfloat16),
    )
    solved, forward_last = lax.fori_loop(0, moments, forward, forward_start)

    def backward(moment, carry):
        moved, outgoing = carry
        incoming = shifted(outgoing, "front", -1)
        panel = moment - (fronts - 1 - front_pos)
        valid = (panel >= 0) & (panel < groups)
        clipped = jnp.clip(panel, 0, groups - 1)

        def backward_active(unused):
            upper = lax.dynamic_index_in_dim(solved, clipped, 0, keepdims=False).astype(jnp.float32)
            reduced = (upper - incoming.astype(jnp.float32)).astype(jnp.bfloat16)
            displaced = jnp.dot(reduced, inverse_block, preferred_element_type=jnp.float32)
            handed = jnp.dot(
                displaced.astype(jnp.bfloat16), coupling_block, preferred_element_type=jnp.float32
            )
            return (displaced, handed.astype(jnp.bfloat16))

        def backward_waiting(unused):
            return (lax.dynamic_index_in_dim(moved, clipped, 0, keepdims=False), outgoing)

        displaced, handed = lax.cond(valid, backward_active, backward_waiting, 0)
        moved = lax.dynamic_update_index_in_dim(moved, displaced, clipped, 0)
        return (moved, handed)

    backward_start = (
        jnp.zeros((groups, width, order), jnp.float32),
        jnp.zeros((width, order), jnp.bfloat16),
    )
    moved, backward_last = lax.fori_loop(0, moments, backward, backward_start)
    displacement = moved.reshape(columns_all, order)
    modal = lax.psum(
        contract_last(displacement.astype(jnp.bfloat16), mode_block).astype(jnp.bfloat16), "front"
    )
    deflated = displacement - jnp.dot(modal, mode_block, preferred_element_type=jnp.float32)
    own_rows = jnp.take(deflated, offsets, axis=1).T
    total_ids = interface_id.shape[0] * columns_all // 2
    dual_ids = jnp.arange(total_ids, dtype=jnp.int32)
    owners = lax.axis_size("sub") * fronts
    share = total_ids // owners
    gathered = lax.all_gather(
        own_rows.astype(jnp.bfloat16), ("sub", "front"), axis=0, tiled=True
    ).astype(own_rows.dtype)
    subs_all = interface_id.shape[0]
    flat_labels = interface_id.reshape(-1)
    owner_pos = sub_pos * fronts + front_pos
    targets = owner_pos * share + jnp.arange(share, dtype=jnp.int32)
    row_select = (targets[:, None] == flat_labels[None, :]).astype(jnp.float32)
    reduced = jnp.einsum(
        "asc,scd->asd",
        row_select.reshape(share, subs_all, columns_all),
        gathered.reshape(subs_all, columns_all, columns_all),
        precision=lax.Precision.HIGHEST,
    )
    column_place = (flat_labels[:, None] == dual_ids[None, :]).astype(jnp.float32)
    flexibility = jnp.dot(
        reduced.reshape(share, subs_all * columns_all),
        column_place,
        precision=lax.Precision.HIGHEST,
    )
    return (deflated.astype(jnp.bfloat16)[None], flexibility)


def solution(mesh):
    return jax.shard_map(
        on_device,
        mesh=mesh,
        in_specs=(
            P("sub", "front", None),
            P("sub", "front", None),
            P("sub", None, "front"),
            P("sub", "front"),
            P(),
        ),
        out_specs=(P("sub", None, "front"), P(("sub", "front"), None)),
        check_vma=False,
    )
```

profile of v0, /device:TPU:0, one launch (start us, length us, event | category | flops | bytes accessed | tf_op | source)
XLA Modules:
  0.0 390.6 jit_solution(3004368580467127556)
XLA Ops:
  7.3 2.6 convolution_bitcast_fusion
  9.8 0.1 broadcast.48.clone
  9.9 126.6 %while.35 = (s32[]{:T(128)}, bf16[1,256,2048]{2,1,0:T(8,128)(2,1)}, bf16[256,2048]{1,0:T(8,128)(2,1)S(1)}, s32[]{:T(128)}, f32[1,256,2048]{2,1,0:T(8,128)}, /*in...) while((s32[]{:T(128)}, bf16[1,256,2048]{2,1,0:T(8,128)(2,1)}, ...), condition=%wide.region_3.4_spmd, body=%wide.region_0.3_spmd.sunk | while | flops 4296540160 | bytes 33554672 | solution.py:66
  10.0 0.1 copy.23
  10.1 5.0 %collective-permute-start = (bf16[256,2048]{1,0:T(8,128)(2,1)S(1)}, bf16[256,2048]{1,0:T(8,128)(2,1)S(1)}, u32[]{:S(2)}, u32[]{:S(2)}) collective-permute-start(bf16[256,2048]{1,0:T(8,128)(2,1)S(1)} %copy.23), channel_id=1, source_target_pairs={{0,1},{1,2},{2,3},{4,5},{5,6},{6,7},{8,9},{9,10},{10,11},{12,13},{... | collective-permute-start | bytes 3145736 | tf_op jit(solution)/shard_map/while/body/eval_jaxpr/ppermute | solution.py:10
  15.1 22.3 %collective-permute-done = bf16[256,2048]{1,0:T(8,128)(2,1)S(1)} collective-permute-done((bf16[256,2048]{1,0:T(8,128)(2,1)S(1)}, bf16[256,2048]{1,0:T(8,128)(2,1)S(1)}, u32[]{:S(2)}, u32[]{:S(2)}) %collective-permute-start) | collective-permute-done | bytes 1048608 | tf_op jit(solution)/shard_map/while/body/eval_jaxpr/ppermute | solution.py:10
  37.4 10.9 %conditional.4 = (bf16[256,2048]{1,0:T(8,128)(2,1)S(1)}) conditional(s32[]{:T(128)} %convert_element_type.98, bf16[256,2048]{1,0:T(8,128)(2,1)S(1)} %copy.23, (f32[1,256,2048]{2,1,0:T(8,128)}, bf16[256,2048]{1,0:T(8,128)(2,1)S(1)}, bf16[2048,2048]{1,0:T(8,128)(2,1)}, bf16[2048,2048]{1,0:T(8,128)(2,1)}) %tuple.101), branch_computations={%region_1.1_spmd, %region_2.2_spmd} | conditional | flops 4296540160 | bytes 20971528 | solution.py:58
  37.4 10.9 %convolution_convert_fusion = bf16[256,2048]{1,0:T(8,128)(2,1)S(1)} fusion(bf16[2048,2048]{1,0:T(8,128)(2,1)} %get-tuple-element.340, bf16[256,2048]{1,0:T(8,128)(2,1)S(1)} %get-tuple-element.338, bf16[2048,2048]{1,0:T(8,128)(2,1)} %get-tuple-element.339, f32[1,256,2048]{2,1,0:T(8,128)} %get-tuple-element.337), kind=kOutput, calls=%fused_computation.3 | convolution fusion | flops 4296540160 | bytes 20971520 | tf_op jit(solution)/shard_map/while/body/eval_jaxpr/cond/branch_1_fun/dot_general | solution.py:14
  48.4 0.1 copy.26
  48.5 0.9 copy-done.1
  49.3 0.1 copy.23
  49.4 1.4 collective-permute-start
  50.8 21.8 %collective-permute-done = bf16[256,2048]{1,0:T(8,128)(2,1)S(1)} collective-permute-done((bf16[256,2048]{1,0:T(8,128)(2,1)S(1)}, bf16[256,2048]{1,0:T(8,128)(2,1)S(1)}, u32[]{:S(2)}, u32[]{:S(2)}) %collective-permute-start) | collective-permute-done | bytes 1048608 | tf_op jit(solution)/shard_map/while/body/eval_jaxpr/ppermute | solution.py:10
  72.6 0.1 copy.26
  72.7 0.9 copy-done.1
  73.5 0.1 copy.23
  73.6 15.4 %collective-permute-start = (bf16[256,2048]{1,0:T(8,128)(2,1)S(1)}, bf16[256,2048]{1,0:T(8,128)(2,1)S(1)}, u32[]{:S(2)}, u32[]{:S(2)}) collective-permute-start(bf16[256,2048]{1,0:T(8,128)(2,1)S(1)} %copy.23), channel_id=1, source_target_pairs={{0,1},{1,2},{2,3},{4,5},{5,6},{6,7},{8,9},{9,10},{10,11},{12,13},{... | collective-permute-start | bytes 3145736 | tf_op jit(solution)/shard_map/while/body/eval_jaxpr/ppermute | solution.py:10
  89.1 20.9 %collective-permute-done = bf16[256,2048]{1,0:T(8,128)(2,1)S(1)} collective-permute-done((bf16[256,2048]{1,0:T(8,128)(2,1)S(1)}, bf16[256,2048]{1,0:T(8,128)(2,1)S(1)}, u32[]{:S(2)}, u32[]{:S(2)}) %collective-permute-start) | collective-permute-done | bytes 1048608 | tf_op jit(solution)/shard_map/while/body/eval_jaxpr/ppermute | solution.py:10
  110.0 0.1 copy.26
  110.1 0.9 copy-done.1
  110.9 0.1 copy.23
  111.0 4.5 %collective-permute-start = (bf16[256,2048]{1,0:T(8,128)(2,1)S(1)}, bf16[256,2048]{1,0:T(8,128)(2,1)S(1)}, u32[]{:S(2)}, u32[]{:S(2)}) collective-permute-start(bf16[256,2048]{1,0:T(8,128)(2,1)S(1)} %copy.23), channel_id=1, source_target_pairs={{0,1},{1,2},{2,3},{4,5},{5,6},{6,7},{8,9},{9,10},{10,11},{12,13},{... | collective-permute-start | bytes 3145736 | tf_op jit(solution)/shard_map/while/body/eval_jaxpr/ppermute | solution.py:10
  115.5 20.0 %collective-permute-done = bf16[256,2048]{1,0:T(8,128)(2,1)S(1)} collective-permute-done((bf16[256,2048]{1,0:T(8,128)(2,1)S(1)}, bf16[256,2048]{1,0:T(8,128)(2,1)S(1)}, u32[]{:S(2)}, u32[]{:S(2)}) %collective-permute-start) | collective-permute-done | bytes 1048608 | tf_op jit(solution)/shard_map/while/body/eval_jaxpr/ppermute | solution.py:10
  135.6 0.9 copy-done.1
  136.5 1.6 broadcast_in_dim.49
  138.1 0.1 broadcast.48
  138.2 144.6 %while.36 = (s32[]{:T(128)}, f32[1,256,2048]{2,1,0:T(8,128)}, bf16[256,2048]{1,0:T(8,128)(2,1)S(1)}, s32[]{:T(128)}, bf16[1,256,2048]{2,1,0:T(8,128)(2,1)S(1)}, ...) while((s32[]{:T(128)}, f32[1,256,2048]{2,1,0:T(8,128)}, ...), condition=%wide.region_7.8_spmd, body=%wide.region_4.7_spmd.sunk | while | flops 4298113024 | bytes 70254888 | solution.py:95
  138.2 1.3 collective-permute-start.1
  139.5 32.5 %collective-permute-done.1 = bf16[256,2048]{1,0:T(8,128)(2,1)} collective-permute-done((bf16[256,2048]{1,0:T(8,128)(2,1)S(1)}, bf16[256,2048]{1,0:T(8,128)(2,1)}, u32[]{:S(2)}, u32[]{:S(2)}) %collective-permute-start.1) | collective-permute-done | bytes 1048608 | tf_op jit(solution)/shard_map/while/body/eval_jaxpr/ppermute | solution.py:10
  172.1 1.3 collective-permute-start.1
  173.4 22.9 %collective-permute-done.1 = bf16[256,2048]{1,0:T(8,128)(2,1)} collective-permute-done((bf16[256,2048]{1,0:T(8,128)(2,1)S(1)}, bf16[256,2048]{1,0:T(8,128)(2,1)}, u32[]{:S(2)}, u32[]{:S(2)}) %collective-permute-start.1) | collective-permute-done | bytes 1048608 | tf_op jit(solution)/shard_map/while/body/eval_jaxpr/ppermute | solution.py:10
  196.3 1.3 collective-permute-start.1
  197.5 31.3 %collective-permute-done.1 = bf16[256,2048]{1,0:T(8,128)(2,1)} collective-permute-done((bf16[256,2048]{1,0:T(8,128)(2,1)S(1)}, bf16[256,2048]{1,0:T(8,128)(2,1)}, u32[]{:S(2)}, u32[]{:S(2)}) %collective-permute-start.1) | collective-permute-done | bytes 1048608 | tf_op jit(solution)/shard_map/while/body/eval_jaxpr/ppermute | solution.py:10
  228.8 1.3 collective-permute-start.1
  230.1 44.1 %collective-permute-done.1 = bf16[256,2048]{1,0:T(8,128)(2,1)} collective-permute-done((bf16[256,2048]{1,0:T(8,128)(2,1)S(1)}, bf16[256,2048]{1,0:T(8,128)(2,1)}, u32[]{:S(2)}, u32[]{:S(2)}) %collective-permute-start.1) | collective-permute-done | bytes 1048608 | tf_op jit(solution)/shard_map/while/body/eval_jaxpr/ppermute | solution.py:10
  274.2 8.5 %conditional.5 = ((bf16[256,2048]{1,0:T(8,128)(2,1)S(1)}, f32[1,256,2048]{2,1,0:T(8,128)})) conditional(s32[]{:T(128)} %convert_element_type.99, (bf16[256,2048]{1,0:T(8,128)(2,1)S(1)}, f32[1,256,2048]{2,1,0:T(8,128)}) %tuple.103, (bf16[1,256,2048]{2,1,0:T(8,128)(2,1)S(1)}, bf16[256,2048]{1,0:T(8,128)(2,1)}, bf16[2048,2048]{1,0:T(8,128)(2,1)}, ...), branch_computations={%region_5.5_spmd, %region_6.6_spmd} | conditional | flops 4298113024 | bytes 66060368 | solution.py:87
  274.2 6.2 %fusion.2 = f32[256,2048]{1,0:T(8,128)S(1)} fusion(bf16[2048,2048]{1,0:T(8,128)(2,1)} %get-tuple-element.350, bf16[256,2048]{1,0:T(8,128)(2,1)} %get-tuple-element.349, bf16[1,256,2048]{2,1,0:T(8,128)(2,1)S(1)} %get-tuple-element.348), kind=kOutput, calls=%fused_computation.7 | convolution fusion | flops 2149580800 | bytes 12582912 | tf_op jit(solution)/shard_map/while/body/eval_jaxpr/cond/branch_1_fun/dot_general | solution.py:78
  280.4 2.3 convolution_convert_fusion.1
  282.8 3.1 fusion.11
  286.0 0.2 all-gather.2.cloned.1.call-start
  286.3 33.1 %all-reduce.2.cloned.1.call-done = bf16[256,300]{1,0:T(8,128)(2,1)} async-done(((bf16[256,300]{1,0:T(8,128)(2,1)}), bf16[256,300]{1,0:T(8,128)(2,1)}) %all-reduce.2.cloned.1.call-update) | async-done | bytes 153616 | tf_op jit(solution)/shard_map/psum | solution.py:97
  319.4 2.6 convolution_subtract_fusion.1
  322.0 1.5 copy.8
  323.5 0.7 gather_fusion
  324.2 0.7 select_convert_fusion
  324.9 53.6 %all-gather.2.cloned.1.call-done = bf16[2048,256]{1,0:T(8,128)(2,1)} async-done(((bf16[64,256]{1,0:T(8,128)(2,1)}), bf16[2048,256]{1,0:T(8,128)(2,1)}) %all-gather.2.cloned.1.call-update) | async-done | bytes 1048592 | tf_op jit(solution)/shard_map/all_gather | solution.py:106
  378.5 1.5 convolution_bitcast_fusion.1
  380.1 3.8 fusion.6
  (36 shorter events, 0.3 us)
Async XLA Ops:
  7.2 275.7 %copy-start = (bf16[1,300,2048]{2,1,0:T(8,128)(2,1)S(1)}, bf16[1,300,2048]{2,1,0:T(8,128)(2,1)}, u32[]{:S(2)}) copy-start(bf16[1,300,2048]{2,1,0:T(8,128)(2,1)} %param.15) | copy-start | bytes 3686404
  7.2 312.2 %all-reduce.2.cloned.1.call-start = ((), (), s32[]{:S(2)}) async-start(), calls=%async_computation | async-start | bytes 393216 | tf_op jit(solution)/shard_map/psum | solution.py:97
  10.1 27.4 %collective-permute-start = (bf16[256,2048]{1,0:T(8,128)(2,1)S(1)}, bf16[256,2048]{1,0:T(8,128)(2,1)S(1)}, u32[]{:S(2)}, u32[]{:S(2)}) collective-permute-start(bf16[256,2048]{1,0:T(8,128)(2,1)S(1)} %copy.23), channel_id=1, source_target_pairs={{0,1},{1,2},{2,3},{4,5},{5,6},{6,7},{8,9},{9,10},{10,11},{12,13},{... | collective-permute-start | bytes 3145736 | tf_op jit(solution)/shard_map/while/body/eval_jaxpr/ppermute | solution.py:10
  48.4 1.0 copy-start.1
  49.4 23.1 %collective-permute-start = (bf16[256,2048]{1,0:T(8,128)(2,1)S(1)}, bf16[256,2048]{1,0:T(8,128)(2,1)S(1)}, u32[]{:S(2)}, u32[]{:S(2)}) collective-permute-start(bf16[256,2048]{1,0:T(8,128)(2,1)S(1)} %copy.23), channel_id=1, source_target_pairs={{0,1},{1,2},{2,3},{4,5},{5,6},{6,7},{8,9},{9,10},{10,11},{12,13},{... | collective-permute-start | bytes 3145736 | tf_op jit(solution)/shard_map/while/body/eval_jaxpr/ppermute | solution.py:10
  72.6 1.0 copy-start.1
  73.6 36.3 %collective-permute-start = (bf16[256,2048]{1,0:T(8,128)(2,1)S(1)}, bf16[256,2048]{1,0:T(8,128)(2,1)S(1)}, u32[]{:S(2)}, u32[]{:S(2)}) collective-permute-start(bf16[256,2048]{1,0:T(8,128)(2,1)S(1)} %copy.23), channel_id=1, source_target_pairs={{0,1},{1,2},{2,3},{4,5},{5,6},{6,7},{8,9},{9,10},{10,11},{12,13},{... | collective-permute-start | bytes 3145736 | tf_op jit(solution)/shard_map/while/body/eval_jaxpr/ppermute | solution.py:10
  110.0 1.0 copy-start.1
  111.0 24.5 %collective-permute-start = (bf16[256,2048]{1,0:T(8,128)(2,1)S(1)}, bf16[256,2048]{1,0:T(8,128)(2,1)S(1)}, u32[]{:S(2)}, u32[]{:S(2)}) collective-permute-start(bf16[256,2048]{1,0:T(8,128)(2,1)S(1)} %copy.23), channel_id=1, source_target_pairs={{0,1},{1,2},{2,3},{4,5},{5,6},{6,7},{8,9},{9,10},{10,11},{12,13},{... | collective-permute-start | bytes 3145736 | tf_op jit(solution)/shard_map/while/body/eval_jaxpr/ppermute | solution.py:10
  135.5 1.0 copy-start.1
  136.5 1.7 copy-start.2
  138.2 33.8 %collective-permute-start.1 = (bf16[256,2048]{1,0:T(8,128)(2,1)S(1)}, bf16[256,2048]{1,0:T(8,128)(2,1)}, u32[]{:S(2)}, u32[]{:S(2)}) collective-permute-start(bf16[256,2048]{1,0:T(8,128)(2,1)S(1)} %get-tuple-element.526), channel_id=1, source_target_pairs={{1,0},{2,1},{3,2},{5,4},{6,5},{7,6},{9,8},{10,9},{11,10},{13,12},{... | collective-permute-start | bytes 3145736 | tf_op jit(solution)/shard_map/while/body/eval_jaxpr/ppermute | solution.py:10
  172.1 24.2 %collective-permute-start.1 = (bf16[256,2048]{1,0:T(8,128)(2,1)S(1)}, bf16[256,2048]{1,0:T(8,128)(2,1)}, u32[]{:S(2)}, u32[]{:S(2)}) collective-permute-start(bf16[256,2048]{1,0:T(8,128)(2,1)S(1)} %get-tuple-element.526), channel_id=1, source_target_pairs={{1,0},{2,1},{3,2},{5,4},{6,5},{7,6},{9,8},{10,9},{11,10},{13,12},{... | collective-permute-start | bytes 3145736 | tf_op jit(solution)/shard_map/while/body/eval_jaxpr/ppermute | solution.py:10
  196.3 32.6 %collective-permute-start.1 = (bf16[256,2048]{1,0:T(8,128)(2,1)S(1)}, bf16[256,2048]{1,0:T(8,128)(2,1)}, u32[]{:S(2)}, u32[]{:S(2)}) collective-permute-start(bf16[256,2048]{1,0:T(8,128)(2,1)S(1)} %get-tuple-element.526), channel_id=1, source_target_pairs={{1,0},{2,1},{3,2},{5,4},{6,5},{7,6},{9,8},{10,9},{11,10},{13,12},{... | collective-permute-start | bytes 3145736 | tf_op jit(solution)/shard_map/while/body/eval_jaxpr/ppermute | solution.py:10
  228.8 45.4 %collective-permute-start.1 = (bf16[256,2048]{1,0:T(8,128)(2,1)S(1)}, bf16[256,2048]{1,0:T(8,128)(2,1)}, u32[]{:S(2)}, u32[]{:S(2)}) collective-permute-start(bf16[256,2048]{1,0:T(8,128)(2,1)S(1)} %get-tuple-element.526), channel_id=1, source_target_pairs={{1,0},{2,1},{3,2},{5,4},{6,5},{7,6},{9,8},{10,9},{11,10},{13,12},{... | collective-permute-start | bytes 3145736 | tf_op jit(solution)/shard_map/while/body/eval_jaxpr/ppermute | solution.py:10
  274.2 6.2 %copy-start.7 = (bf16[2048,2048]{1,0:T(8,128)(2,1)S(1)}, bf16[2048,2048]{1,0:T(8,128)(2,1)}, u32[]{:S(2)}) copy-start(bf16[2048,2048]{1,0:T(8,128)(2,1)} %get-tuple-element.351) | copy-start | bytes 25165828 | tf_op jit(solution)/shard_map/while/body/eval_jaxpr/cond
  280.4 2.4 copy-start.3
  282.8 3.4 copy-start.6
  282.8 36.5 %copy-start.4 = (f32[1,256,2048]{2,1,0:T(8,128)S(1)}, f32[1,256,2048]{2,1,0:T(8,128)}, u32[]{:S(2)}) copy-start(f32[1,256,2048]{2,1,0:T(8,128)} %get-tuple-element.367) | copy-start | bytes 6291460
  286.0 92.5 %all-gather.2.cloned.1.call-start = ((), (), s32[]{:S(2)}) async-start(), calls=%async_computation.1 | async-start | bytes 1081344 | tf_op jit(solution)/shard_map/all_gather | solution.py:106
  322.0 2.9 copy-start.5
Sparse Core Ops, SparseCore 0:
  286.1 33.1 all-reduce.1
  325.0 53.4 all-gather.1
where the time goes:
time: 391 us
  waiting for transfers between devices  302 us (77%)
  matrix products  33 us (8%)
  starting transfers between devices  31.6 us (8%)
  between operations  14.2 us (4%)
  local copies, waits for them, and re-layouts  8.29 us (2%)
    ppermute x8, waiting for transfers between devices, shifted(): lax.ppermute(value, axis, [(source, source + steps) for source in range(l...  216 us
    all_gather x1, waiting for transfers between devices, on_device(): lax.all_gather(own_rows.astype(jnp.bfloat16), ('sub', 'front'), axis=0, t...  53.6 us
    psum x1, waiting for transfers between devices, on_device(): lax.psum(contract_last(displacement.astype(jnp.bfloat16), mode_block).ast...  33.1 us
    ppermute x8, starting transfers between devices, shifted(): lax.ppermute(value, axis, [(source, source + steps) for source in range(l...  31.4 us
    dot_general x2, matrix products, contract_last(): lax.dot_general(left, right, (((1,), (1,)), ((), ())), preferred_element_...  14.1 us
  transfers between devices with their start and end apart: 10, of which 10 were waited for; matrix products, arithmetic and copies ran while one was open for 0% of the time, Pallas kernels for 0%

commit v1 on v0

v1 whole, which is shorter than its diff:
```python
import functools

import jax
import jax.numpy as jnp
from jax import lax
from jax.experimental import pallas as pl
from jax.experimental.pallas import tpu as pltpu
from jax.sharding import PartitionSpec as P

VMEM = pl.BlockSpec(memory_space=pltpu.VMEM)
SMEM = pl.BlockSpec(memory_space=pltpu.SMEM)
HBM = pl.BlockSpec(memory_space=pltpu.HBM)
GRANT = 18 << 20
BF16 = jnp.bfloat16
F32 = jnp.float32


def contract_last(left, right):
    return lax.dot_general(left, right, (((1,), (1,)), ((), ())), preferred_element_type=F32)


def tiles(total):
    width = 1024 if total % 1024 == 0 else total
    return [slice(start, start + width) for start in range(0, total, width)]


def call(body, outs, name):
    return functools.partial(
        pl.pallas_call,
        body,
        out_shape=outs,
        name=name,
        compiler_params=pltpu.CompilerParams(vmem_limit_bytes=GRANT),
    )


def hold(value):
    return pltpu.with_memory_space_constraint(value, pltpu.VMEM)


def column_of(row):
    count = row.shape[1]
    square = (count, count)
    same = lax.broadcasted_iota(jnp.int32, square, 0) == lax.broadcasted_iota(jnp.int32, square, 1)
    spread = jnp.where(same, jnp.broadcast_to(row, square).astype(F32), 0.0)
    return jnp.sum(spread, axis=1, keepdims=True).astype(jnp.int32)


def unit_rows(offsets, order):
    rows = lax.broadcasted_iota(jnp.int32, (offsets.shape[1], order), 1)
    return (rows == column_of(offsets)).astype(BF16)


def own_panel(offsets, inverse):
    count, order = offsets.shape[1], inverse.shape[0]
    cuts = tiles(order)

    def body(offsets_ref, inverse_ref, out_ref, held_ref, arrived):
        copies = [
            pltpu.make_async_copy(inverse_ref.at[cut, :], held_ref.at[cut, :], arrived.at[index])
            for index, cut in enumerate(cuts)
        ]
        for copy in copies:
            copy.start()
        pick = unit_rows(offsets_ref[...], order)
        for copy, cut in zip(copies, cuts):
            copy.wait()
            out_ref[:, cut] = contract_last(pick, held_ref[cut, :]).astype(BF16)

    outs = (jax.ShapeDtypeStruct((count, order), BF16), pltpu.VMEM(inverse.shape, BF16))
    return call(body, outs, "own_panel")(
        in_specs=[VMEM, HBM],
        out_specs=(VMEM, VMEM),
        scratch_shapes=[pltpu.SemaphoreType.DMA((len(cuts),))],
    )(offsets, inverse)


def bring(block):
    def body(block_ref, held_ref, arrived):
        copy = pltpu.make_async_copy(block_ref, held_ref, arrived)
        copy.start()
        copy.wait()

    return call(body, pltpu.VMEM(block.shape, block.dtype), "bring")(
        in_specs=[HBM],
        out_specs=VMEM,
        scratch_shapes=[pltpu.SemaphoreType.DMA],
    )(block)


def forward_step(moment, handed, coupling, inverse):
    count, order = handed.shape

    def body(handed_ref, coupling_ref, inverse_ref, out_ref, reduced_ref):
        @pl.when(lax.axis_index("front") >= moment)
        def _():
            for cut in tiles(order):
                reduced_ref[:, cut] = (-contract_last(handed_ref[...], coupling_ref[cut, :])).astype(BF16)
            for cut in tiles(order):
                out_ref[:, cut] = contract_last(reduced_ref[...], inverse_ref[cut, :]).astype(BF16)

    return call(body, jax.ShapeDtypeStruct((count, order), BF16), "forward_step")(
        in_specs=[VMEM, VMEM, VMEM],
        out_specs=VMEM,
        scratch_shapes=[pltpu.VMEM((count, order), BF16)],
    )(handed, hold(coupling), hold(inverse))


def backward_step(moment, fronts, solved, handed, coupling, inverse):
    count, order = solved[0].shape
    last = fronts - 1
    final = moment == 2 * last

    def body(*refs):
        refs = list(refs)
        solved_refs = [refs.pop(0) for _ in solved]
        handed_ref = refs.pop(0) if handed is not None else None
        coupling_ref = None if final else refs.pop(0)
        inverse_ref = refs.pop(0)
        moved_ref = refs.pop(0)
        out_ref = None if final else refs.pop(0)
        back_ref = refs.pop(0)
        front = lax.axis_index("front")
        panel = 2 * last - front - moment

        @pl.when((panel >= 0) & (panel < fronts))
        def _():
            if handed_ref is None:
                back_ref[...] = jnp.zeros_like(back_ref)
            else:
                back_ref[...] = -handed_ref[...]
            for index, ref in enumerate(solved_refs):

                @pl.when(front - panel == index)
                def _(ref=ref):
                    back_ref[...] = (back_ref[...].astype(F32) + ref[...].astype(F32)).astype(BF16)

            for cut in tiles(order):
                moved_ref[:, cut] = jnp.dot(back_ref[...], inverse_ref[:, cut], preferred_element_type=F32)
            if not final:
                back_ref[...] = moved_ref[...].astype(BF16)
                for cut in tiles(order):
                    out_ref[:, cut] = jnp.dot(
                        back_ref[...], coupling_ref[:, cut], preferred_element_type=F32
                    ).astype(BF16)

    operands = list(solved)
    if handed is not None:
        operands.append(handed)
    if not final:
        operands.append(hold(coupling))
    operands.append(hold(inverse))
    outs = [jax.ShapeDtypeStruct((count, order), F32)]
    if not final:
        outs.append(jax.ShapeDtypeStruct((count, order), BF16))
    return call(body, outs, "backward_step")(
        in_specs=[VMEM] * len(operands),
        out_specs=[VMEM] * len(outs),
        scratch_shapes=[pltpu.VMEM((count, order), BF16)],
    )(*operands)


def project(moved, modes, fronts):
    count, order = moved[0].shape
    free = modes.shape[0]
    last = fronts - 1

    def body(*refs):
        moved_refs, (modes_ref, all_ref, modal_ref, sent_ref) = refs[: len(moved)], refs[len(moved) :]
        front = lax.axis_index("front")
        for moment, ref in enumerate(moved_refs):
            panel = 2 * last - front - moment

            @pl.when((panel >= 0) & (panel < fronts))
            def _(ref=ref, panel=panel):
                all_ref[pl.ds(pl.multiple_of(panel * count, count), count), :] = ref[...]

        modal = contract_last(all_ref[...].astype(BF16), modes_ref[...])
        modal_ref[...] = modal
        sent_ref[...] = modal.astype(BF16)

    rows = fronts * count
    outs = [
        jax.ShapeDtypeStruct((rows, order), F32),
        jax.ShapeDtypeStruct((rows, free), F32),
        jax.ShapeDtypeStruct((rows, free), BF16),
    ]
    return call(body, outs, "project")(
        in_specs=[VMEM] * (len(moved) + 1), out_specs=[VMEM] * 3
    )(*moved, modes)


def add_other(value, other):
    def body(value_ref, other_ref, sum_ref, sent_ref):
        total = value_ref[...] + other_ref[...].astype(F32)
        sum_ref[...] = total
        sent_ref[...] = total.astype(BF16)

    outs = [jax.ShapeDtypeStruct(value.shape, F32), jax.ShapeDtypeStruct(value.shape, BF16)]
    return call(body, outs, "add_other")(in_specs=[VMEM] * 2, out_specs=[VMEM] * 2)(value, other)


def deflate(displacement, modal, modes, offsets):
    rows, order = displacement.shape

    def body(displacement_ref, modal_ref, modes_ref, offsets_ref, out_ref, picked_ref):
        for cut in tiles(order):
            left = jnp.dot(modal_ref[...], modes_ref[:, cut], preferred_element_type=F32)
            out_ref[:, cut] = (displacement_ref[:, cut] - left).astype(BF16)
        pick = unit_rows(offsets_ref[...], order)
        picked_ref[...] = contract_last(pick, out_ref[...]).astype(BF16)

    outs = [
        jax.ShapeDtypeStruct((rows, order), BF16),
        jax.ShapeDtypeStruct((offsets.shape[1], rows), BF16),
    ]
    return call(body, outs, "deflate")(in_specs=[VMEM] * 4, out_specs=[VMEM] * 2)(
        displacement, modal, modes, offsets
    )


def exchange_rows(value, axis):
    count = lax.axis_size(axis)
    value = value[None]
    step = 1
    while step < count:
        other = lax.ppermute(value, axis, [(i, i ^ step) for i in range(count)])
        value = jnp.concatenate([value, other])
        step *= 2
    return value


def assemble(gathered, interface_id, share):
    subs, fronts, per_front, columns = gathered.shape
    total = subs * columns // 2

    def body(gathered_ref, ids_ref, out_ref):
        sub_here, front_here = lax.axis_index("sub"), lax.axis_index("front")
        first = (sub_here * fronts + front_here) * share
        targets = first + lax.broadcasted_iota(jnp.int32, (share, columns), 0)
        holder = lax.broadcasted_iota(jnp.int32, (share, columns), 1) // per_front
        dual = lax.broadcasted_iota(jnp.int32, (total, columns), 0)
        flexibility = jnp.zeros((share, total), F32)
        for sub_step in range(subs):
            ids = ids_ref[pl.ds(sub_here ^ sub_step, 1), :]
            hit = targets == ids
            reduced = jnp.zeros((share, columns), F32)
            for front_step in range(fronts):
                front = front_here ^ front_step
                rows = hit & (holder == front)
                chosen = rows.astype(BF16)
                block = gathered_ref[sub_step, front_step]
                tall = jnp.concatenate([block] * fronts, axis=0)
                reduced = reduced + jnp.dot(chosen, tall, preferred_element_type=F32)
            place = (dual == ids).astype(BF16)
            flexibility = flexibility + contract_last(reduced.astype(BF16), place)
        out_ref[...] = flexibility

    return call(body, jax.ShapeDtypeStruct((share, total), F32), "assemble")(
        in_specs=[VMEM] * 2, out_specs=VMEM
    )(gathered, interface_id)


def on_device(front_inverse, coupling, free_modes, dof_offset, interface_id):
    inverse_block = front_inverse[0]
    coupling_block = coupling[0]
    mode_block = free_modes[0]
    subs_all, columns_all = interface_id.shape
    fronts = lax.axis_size("front")

    own, inverse_block = own_panel(dof_offset, inverse_block)
    coupling_block = bring(coupling_block)
    solved = [own]
    moved = []
    arriving = None
    last = fronts - 1
    for moment in range(2 * fronts - 1):
        if 0 < moment < fronts:
            pairs = [(i, i + 1) for i in range(moment - 1, last)]
            handed = lax.ppermute(solved[-1], "front", pairs)
            solved.append(forward_step(moment, handed, coupling_block, inverse_block))
        outcome = backward_step(moment, fronts, solved, arriving, coupling_block, inverse_block)
        moved.append(outcome[0])
        if moment < 2 * last:
            pairs = [(i, i - 1) for i in range(1, fronts) if last - moment <= i <= 2 * last - moment]
            arriving = lax.ppermute(outcome[1], "front", pairs)

    displacement, modal, sent = project(moved, mode_block, fronts)
    step = 1
    while step < fronts:
        other = lax.ppermute(sent, "front", [(i, i ^ step) for i in range(fronts)])
        modal, sent = add_other(modal, other)
        step *= 2
    deflated, own_rows = deflate(displacement, sent, mode_block, dof_offset)
    gathered = exchange_rows(exchange_rows(own_rows, "front"), "sub")
    share = subs_all * columns_all // 2 // (lax.axis_size("sub") * fronts)
    return (deflated[None], assemble(gathered, interface_id, share))


def solution(mesh):
    return jax.shard_map(
        on_device,
        mesh=mesh,
        in_specs=(
            P("sub", "front", None),
            P("sub", "front", None),
            P("sub", None, "front"),
            P("sub", "front"),
            P(),
        ),
        out_specs=(P("sub", None, "front"), P(("sub", "front"), None)),
        check_vma=False,
    )
```

time: 391 us -> 146 us (0.37)
  waiting for transfers between devices: 302 us -> 102 us
  matrix products: 33 us -> 0 us
  Pallas kernels: 0 us -> 22.4 us
  starting transfers between devices: 31.6 us -> 16.3 us
  between operations: 14.2 us -> 0.93 us
  local copies, waits for them, and re-layouts: 8.29 us -> 4.05 us
    ppermute x8 -> x16, waiting for transfers between devices: 216 us -> 102 us  [the longest x6 52.4 us: on_device(): arriving = lax.ppermute(outcome[1], 'front', pairs)]
    all_gather x1 -> x0, waiting for transfers between devices: 53.6 us -> none  [on_device(): lax.all_gather(own_rows.astype(jnp.bfloat16), ('sub', 'front'), axis=0, t...]
    psum x1 -> x0, waiting for transfers between devices: 33.1 us -> none  [on_device(): lax.psum(contract_last(displacement.astype(jnp.bfloat16), mode_block).ast...]
    dot_general x8 -> x0, matrix products: 33 us -> none  [the longest x2 14.1 us: contract_last(): lax.dot_general(left, right, (((1,), (1,)), ((), ())), preferred_element_...]
    pallas_call x0 -> x17, Pallas kernels: none -> 22.4 us  [the longest x7 11.2 us: backward_step(): call(body, outs, 'backward_step')]
    ppermute x8 -> x16, starting transfers between devices: 31.4 us -> 16.3 us  [the longest x6 6.65 us: on_device(): arriving = lax.ppermute(outcome[1], 'front', pairs)]
    unnamed x11 -> x12, local copies, waits for them, and re-layouts: 0.03 us -> 4.05 us
  transfers between devices with their start and end apart: 10 -> 16, of which waited for: 10 -> 12; matrix products, arithmetic and copies ran while one was open for 0% -> 0% of each run, Pallas kernels for 0% -> 1%
where the time goes in v1:
time: 146 us
  waiting for transfers between devices  102 us (70%)
  Pallas kernels  22.4 us (15%)
  starting transfers between devices  16.3 us (11%)
  local copies, waits for them, and re-layouts  4.05 us (3%)
    ppermute x6, waiting for transfers between devices, on_device(): arriving = lax.ppermute(outcome[1], 'front', pairs)  52.4 us
    ppermute x5, waiting for transfers between devices, exchange_rows(): other = lax.ppermute(value, axis, [(i, i ^ step) for i in range(count)])  29.1 us
    ppermute x2, waiting for transfers between devices, on_device(): other = lax.ppermute(sent, 'front', [(i, i ^ step) for i in range(fronts)])  16.4 us
    pallas_call x7, Pallas kernels, backward_step(): call(body, outs, 'backward_step')  11.2 us
    ppermute x6, starting transfers between devices, on_device(): arriving = lax.ppermute(outcome[1], 'front', pairs)  6.65 us
    ppermute x3, starting transfers between devices, on_device(): handed = lax.ppermute(solved[-1], 'front', pairs)  6.31 us
    ppermute x3, waiting for transfers between devices, on_device(): handed = lax.ppermute(solved[-1], 'front', pairs)  4.24 us
    unnamed x12, local copies, waits for them, and re-layouts  4.05 us
  transfers between devices with their start and end apart: 16, of which 12 were waited for; matrix products, arithmetic and copies ran while one was open for 0% of the time, Pallas kernels for 1%

profile of v1, /device:TPU:0, one launch (start us, length us, event | category | flops | bytes accessed | tf_op | source)
XLA Modules:
  0.0 146.0 jit_solution(5236401533320189894)
XLA Ops:
  0.6 3.4 %copy-done = bf16[1,2048,2048]{2,1,0:T(8,128)(2,1)S(1)} copy-done((bf16[1,2048,2048]{2,1,0:T(8,128)(2,1)S(1)}, bf16[1,2048,2048]{2,1,0:T(8,128)(2,1)}, u32[]{:S(2)}) %copy-start) | copy-done | bytes 8388632
  4.0 0.7 copy-done.4
  4.7 3.5 %own_panel.1 = (bf16[64,2048]{1,0:T(8,128)(2,1)S(1)}, bf16[2048,2048]{1,0:T(8,128)(2,1)S(1)}) custom-call(s32[1,64]{1,0:T(1,128)S(1)} %copy-done.4, bf16[2048,2048]{1,0:T(8,128)(2,1)S(1)} %bitcast.7), custom_call_target="tpu_custom_call" | custom-call | tf_op jit(solution)/shard_map/own_panel/pallas_call | solution.py:71
  8.2 5.0 %collective-permute-start = (bf16[64,2048]{1,0:T(8,128)(2,1)S(1)}, bf16[64,2048]{1,0:T(8,128)(2,1)S(1)}, u32[]{:S(2)}, u32[]{:S(2)}) collective-permute-start(bf16[64,2048]{1,0:T(8,128)(2,1)S(1)} %get-tuple-element.24.refs_0_), channel_id=1, source_target_pairs={{0,1},{1,2},{2,3},{4,5},{5,6},{6,7},{8,9},{9,10},{10,11},{12,13},{... | collective-permute-start | bytes 786440 | tf_op jit(solution)/shard_map/ppermute | solution.py:280
  13.1 0.6 bring.1.refs_1_.coupling_ref.refs_3_.refs_4_.refs_5_
  13.7 0.7 collective-permute-start.1
  14.4 4.2 %collective-permute-done.handed_ref = bf16[64,2048]{1,0:T(8,128)(2,1)S(1)} collective-permute-done((bf16[64,2048]{1,0:T(8,128)(2,1)S(1)}, bf16[64,2048]{1,0:T(8,128)(2,1)S(1)}, u32[]{:S(2)}, u32[]{:S(2)}) %collective-permute-start) | collective-permute-done | bytes 262176 | tf_op jit(solution)/shard_map/ppermute | solution.py:280
  18.7 0.7 collective-permute-start.2
  19.3 0.0 collective-permute-done.1.refs_2_
  19.4 0.7 collective-permute-start.3
  20.1 0.2 forward_step.4.refs_2_
  20.3 0.7 collective-permute-start.4
  21.0 0.0 collective-permute-done.3.refs_3_
  21.0 1.3 collective-permute-start.5
  22.3 28.8 %collective-permute-done.5.refs_4_ = bf16[64,2048]{1,0:T(8,128)(2,1)S(1)} collective-permute-done((bf16[64,2048]{1,0:T(8,128)(2,1)S(1)}, bf16[64,2048]{1,0:T(8,128)(2,1)S(1)}, u32[]{:S(2)}, u32[]{:S(2)}) %collective-permute-start.5) | collective-permute-done | bytes 262176 | tf_op jit(solution)/shard_map/ppermute | solution.py:286
  51.1 3.1 %backward_step.10 = (f32[64,2048]{1,0:T(8,128)S(1)}, bf16[64,2048]{1,0:T(8,128)(2,1)S(1)}) custom-call(bf16[64,2048]{1,0:T(8,128)(2,1)S(1)} %get-tuple-element.24.refs_0_, bf16[64,2048]{1,0:T(8,128)(2,1)S(1)} %forward_step.3.refs_1_, bf16[64,2048]{1,0:T(8,128)(2,1)S(1)} %forward_step.4.refs_2_, bf16[64,2048]{1,0:T(8,128)(2,1)S(1)} %forward_step.5.refs_3_, ...), custom_call_target="tpu_custom_call" | custom-call | tf_op jit(solution)/shard_map/backward_step/pallas_call | solution.py:156
  54.2 1.3 collective-permute-start.6
  55.5 9.2 %collective-permute-done.6.refs_4_ = bf16[64,2048]{1,0:T(8,128)(2,1)S(1)} collective-permute-done((bf16[64,2048]{1,0:T(8,128)(2,1)S(1)}, bf16[64,2048]{1,0:T(8,128)(2,1)S(1)}, u32[]{:S(2)}, u32[]{:S(2)}) %collective-permute-start.6) | collective-permute-done | bytes 262176 | tf_op jit(solution)/shard_map/ppermute | solution.py:286
  64.7 3.3 %backward_step.11 = (f32[64,2048]{1,0:T(8,128)S(1)}, bf16[64,2048]{1,0:T(8,128)(2,1)S(1)}) custom-call(bf16[64,2048]{1,0:T(8,128)(2,1)S(1)} %get-tuple-element.24.refs_0_, bf16[64,2048]{1,0:T(8,128)(2,1)S(1)} %forward_step.3.refs_1_, bf16[64,2048]{1,0:T(8,128)(2,1)S(1)} %forward_step.4.refs_2_, bf16[64,2048]{1,0:T(8,128)(2,1)S(1)} %forward_step.5.refs_3_, ...), custom_call_target="tpu_custom_call" | custom-call | tf_op jit(solution)/shard_map/backward_step/pallas_call | solution.py:156
  68.0 1.3 collective-permute-start.7
  69.3 7.0 %collective-permute-done.7.refs_4_ = bf16[64,2048]{1,0:T(8,128)(2,1)S(1)} collective-permute-done((bf16[64,2048]{1,0:T(8,128)(2,1)S(1)}, bf16[64,2048]{1,0:T(8,128)(2,1)S(1)}, u32[]{:S(2)}, u32[]{:S(2)}) %collective-permute-start.7) | collective-permute-done | bytes 262176 | tf_op jit(solution)/shard_map/ppermute | solution.py:286
  76.3 3.1 %backward_step.12 = (f32[64,2048]{1,0:T(8,128)S(1)}, bf16[64,2048]{1,0:T(8,128)(2,1)S(1)}) custom-call(bf16[64,2048]{1,0:T(8,128)(2,1)S(1)} %get-tuple-element.24.refs_0_, bf16[64,2048]{1,0:T(8,128)(2,1)S(1)} %forward_step.3.refs_1_, bf16[64,2048]{1,0:T(8,128)(2,1)S(1)} %forward_step.4.refs_2_, bf16[64,2048]{1,0:T(8,128)(2,1)S(1)} %forward_step.5.refs_3_, ...), custom_call_target="tpu_custom_call" | custom-call | tf_op jit(solution)/shard_map/backward_step/pallas_call | solution.py:156
  79.4 0.0 copy-start.2
  79.4 0.0 copy-start.5
  79.5 1.4 collective-permute-start.8
  80.9 7.3 %collective-permute-done.8.refs_4_ = bf16[64,2048]{1,0:T(8,128)(2,1)S(1)} collective-permute-done((bf16[64,2048]{1,0:T(8,128)(2,1)S(1)}, bf16[64,2048]{1,0:T(8,128)(2,1)S(1)}, u32[]{:S(2)}, u32[]{:S(2)}) %collective-permute-start.8) | collective-permute-done | bytes 262176 | tf_op jit(solution)/shard_map/ppermute | solution.py:286
  88.2 1.7 %backward_step.13.refs_6_ = f32[64,2048]{1,0:T(8,128)S(1)} custom-call(bf16[64,2048]{1,0:T(8,128)(2,1)S(1)} %get-tuple-element.24.refs_0_, bf16[64,2048]{1,0:T(8,128)(2,1)S(1)} %forward_step.3.refs_1_, bf16[64,2048]{1,0:T(8,128)(2,1)S(1)} %forward_step.4.refs_2_, bf16[64,2048]{1,0:T(8,128)(2,1)S(1)} %forward_step.5.refs_3_, ...), custom_call_target="tpu_custom_call" | custom-call | tf_op jit(solution)/shard_map/backward_step/pallas_call | solution.py:156
  89.9 0.0 copy-start.3
  89.9 0.9 project.1
  90.8 0.1 collective-permute-start.9
  90.9 7.7 %collective-permute-done.9.other_ref = bf16[256,300]{1,0:T(8,128)(2,1)S(1)} collective-permute-done((bf16[256,300]{1,0:T(8,128)(2,1)S(1)}, bf16[256,300]{1,0:T(8,128)(2,1)S(1)}, u32[]{:S(2)}, u32[]{:S(2)}) %collective-permute-start.9) | collective-permute-done | bytes 153632 | tf_op jit(solution)/shard_map/ppermute | solution.py:291
  98.6 0.1 add_other.2
  98.6 0.1 collective-permute-start.10
  98.7 8.8 %collective-permute-done.10.other_ref = bf16[256,300]{1,0:T(8,128)(2,1)S(1)} collective-permute-done((bf16[256,300]{1,0:T(8,128)(2,1)S(1)}, bf16[256,300]{1,0:T(8,128)(2,1)S(1)}, u32[]{:S(2)}, u32[]{:S(2)}) %collective-permute-start.10) | collective-permute-done | bytes 153632 | tf_op jit(solution)/shard_map/ppermute | solution.py:291
  107.5 0.8 add_other.3
  108.3 1.9 %deflate.1 = (bf16[256,2048]{1,0:T(8,128)(2,1)}, bf16[64,256]{1,0:T(8,128)(2,1)S(1)}) custom-call(f32[256,2048]{1,0:T(8,128)S(1)} %get-tuple-element.38.displacement_ref, bf16[256,300]{1,0:T(8,128)(2,1)S(1)} %get-tuple-element.43.modal_ref, bf16[300,2048]{1,0:T(8,128)(2,1)S(1)} %bitcast.10, s32[1,64]{1,0:T(1,128)S(1)} %copy-done.5), custom_call_target="tpu_custom_call" | custom-call | tf_op jit(solution)/shard_map/deflate/pallas_call | solution.py:217
  110.2 3.9 %collective-permute-done.11 = bf16[1,64,256]{2,1,0:T(8,128)(2,1)S(1)} collective-permute-done((bf16[1,64,256]{2,1,0:T(8,128)(2,1)S(1)}, bf16[1,64,256]{2,1,0:T(8,128)(2,1)S(1)}, u32[]{:S(2)}, u32[]{:S(2)}) %collective-permute-start.11) | collective-permute-done | bytes 32800 | tf_op jit(solution)/shard_map/ppermute | solution.py:227
  114.1 0.1 collective-permute-start.12
  114.2 5.3 %collective-permute-done.12 = bf16[2,64,256]{2,1,0:T(8,128)(2,1)S(1)} collective-permute-done((bf16[2,64,256]{2,1,0:T(8,128)(2,1)S(1)}, bf16[2,64,256]{2,1,0:T(8,128)(2,1)S(1)}, u32[]{:S(2)}, u32[]{:S(2)}) %collective-permute-start.12) | collective-permute-done | bytes 65568 | tf_op jit(solution)/shard_map/ppermute | solution.py:227
  119.5 0.1 collective-permute-start.13
  119.6 1.3 collective-permute-done.13
  120.9 1.5 %collective-permute-start.14 = (bf16[2,4,64,256]{3,2,1,0:T(8,128)(2,1)S(1)}, bf16[2,4,64,256]{3,2,1,0:T(8,128)(2,1)S(1)}, u32[]{:S(2)}, u32[]{:S(2)}) collective-permute-start(bf16[2,4,64,256]{3,2,1,0:T(8,128)(2,1)S(1)} %pad_maximum_fusion.2), channel_id=1, source_target_pairs={{0,8},{4,12},{8,0},{12,4},{16,24},{20,28},{24,16},{28,20},{1,9},{5... | collective-permute-start | bytes 786440 | tf_op jit(solution)/shard_map/ppermute | solution.py:227
  122.5 6.9 %collective-permute-done.14 = bf16[2,4,64,256]{3,2,1,0:T(8,128)(2,1)S(1)} collective-permute-done((bf16[2,4,64,256]{3,2,1,0:T(8,128)(2,1)S(1)}, bf16[2,4,64,256]{3,2,1,0:T(8,128)(2,1)S(1)}, u32[]{:S(2)}, u32[]{:S(2)}) %collective-permute-start.14) | collective-permute-done | bytes 262176 | tf_op jit(solution)/shard_map/ppermute | solution.py:227
  129.3 0.1 pad_maximum_fusion.1
  129.4 1.6 %collective-permute-start.15 = (bf16[4,4,64,256]{3,2,1,0:T(8,128)(2,1)S(1)}, bf16[4,4,64,256]{3,2,1,0:T(8,128)(2,1)S(1)}, u32[]{:S(2)}, u32[]{:S(2)}) collective-permute-start(bf16[4,4,64,256]{3,2,1,0:T(8,128)(2,1)S(1)} %pad_maximum_fusion.1), channel_id=1, source_target_pairs={{0,16},{4,20},{8,24},{12,28},{16,0},{20,4},{24,8},{28,12},{1,17},{... | collective-permute-start | bytes 1572872 | tf_op jit(solution)/shard_map/ppermute | solution.py:227
  131.0 11.6 %collective-permute-done.15 = bf16[4,4,64,256]{3,2,1,0:T(8,128)(2,1)S(1)} collective-permute-done((bf16[4,4,64,256]{3,2,1,0:T(8,128)(2,1)S(1)}, bf16[4,4,64,256]{3,2,1,0:T(8,128)(2,1)S(1)}, u32[]{:S(2)}, u32[]{:S(2)}) %collective-permute-start.15) | collective-permute-done | bytes 524320 | tf_op jit(solution)/shard_map/ppermute | solution.py:227
  142.6 0.1 pad_maximum_fusion.gathered_ref
  142.7 3.3 %assemble.1 = f32[32,1024]{1,0:T(8,128)} custom-call(bf16[8,4,64,256]{3,2,1,0:T(8,128)(2,1)S(1)} %pad_maximum_fusion.gathered_ref, s32[8,256]{1,0:T(8,128)S(1)} %copy-done.3), custom_call_target="tpu_custom_call" | custom-call | tf_op jit(solution)/shard_map/assemble/pallas_call | solution.py:259
  (18 shorter events, 0.1 us)
Async XLA Ops:
  0.6 3.4 %copy-start = (bf16[1,2048,2048]{2,1,0:T(8,128)(2,1)S(1)}, bf16[1,2048,2048]{2,1,0:T(8,128)(2,1)}, u32[]{:S(2)}) copy-start(bf16[1,2048,2048]{2,1,0:T(8,128)(2,1)} %param.5) | copy-start | bytes 25165828
  4.0 0.7 copy-start.4
  4.7 8.5 %copy-start.1 = (bf16[1,2048,2048]{2,1,0:T(8,128)(2,1)S(1)}, bf16[1,2048,2048]{2,1,0:T(8,128)(2,1)}, u32[]{:S(2)}) copy-start(bf16[1,2048,2048]{2,1,0:T(8,128)(2,1)} %param.6) | copy-start | bytes 25165828
  8.2 10.5 %collective-permute-start = (bf16[64,2048]{1,0:T(8,128)(2,1)S(1)}, bf16[64,2048]{1,0:T(8,128)(2,1)S(1)}, u32[]{:S(2)}, u32[]{:S(2)}) collective-permute-start(bf16[64,2048]{1,0:T(8,128)(2,1)S(1)} %get-tuple-element.24.refs_0_), channel_id=1, source_target_pairs={{0,1},{1,2},{2,3},{4,5},{5,6},{6,7},{8,9},{9,10},{10,11},{12,13},{... | collective-permute-start | bytes 786440 | tf_op jit(solution)/shard_map/ppermute | solution.py:280
  13.7 5.6 %collective-permute-start.1 = (bf16[64,2048]{1,0:T(8,128)(2,1)S(1)}, bf16[64,2048]{1,0:T(8,128)(2,1)S(1)}, u32[]{:S(2)}, u32[]{:S(2)}) collective-permute-start(bf16[64,2048]{1,0:T(8,128)(2,1)S(1)} %get-tuple-element.27), channel_id=1, source_target_pairs={{3,2},{7,6},{11,10},{15,14},{19,18},{23,22},{27,26},{31,30}} | collective-permute-start | bytes 786440 | tf_op jit(solution)/shard_map/ppermute | solution.py:286
  18.7 1.4 collective-permute-start.2
  19.4 1.6 %collective-permute-start.3 = (bf16[64,2048]{1,0:T(8,128)(2,1)S(1)}, bf16[64,2048]{1,0:T(8,128)(2,1)S(1)}, u32[]{:S(2)}, u32[]{:S(2)}) collective-permute-start(bf16[64,2048]{1,0:T(8,128)(2,1)S(1)} %get-tuple-element.29), channel_id=1, source_target_pairs={{2,1},{3,2},{6,5},{7,6},{10,9},{11,10},{14,13},{15,14},{18,17},{19... | collective-permute-start | bytes 786440 | tf_op jit(solution)/shard_map/ppermute | solution.py:286
  20.3 2.0 %collective-permute-start.4 = (bf16[64,2048]{1,0:T(8,128)(2,1)S(1)}, bf16[64,2048]{1,0:T(8,128)(2,1)S(1)}, u32[]{:S(2)}, u32[]{:S(2)}) collective-permute-start(bf16[64,2048]{1,0:T(8,128)(2,1)S(1)} %forward_step.4.refs_2_), channel_id=1, source_target_pairs={{2,3},{6,7},{10,11},{14,15},{18,19},{22,23},{26,27},{30,31}} | collective-permute-start | bytes 786440 | tf_op jit(solution)/shard_map/ppermute | solution.py:280
  21.0 30.1 %collective-permute-start.5 = (bf16[64,2048]{1,0:T(8,128)(2,1)S(1)}, bf16[64,2048]{1,0:T(8,128)(2,1)S(1)}, u32[]{:S(2)}, u32[]{:S(2)}) collective-permute-start(bf16[64,2048]{1,0:T(8,128)(2,1)S(1)} %get-tuple-element.31), channel_id=1, source_target_pairs={{1,0},{2,1},{3,2},{5,4},{6,5},{7,6},{9,8},{10,9},{11,10},{13,12},{... | collective-permute-start | bytes 786440 | tf_op jit(solution)/shard_map/ppermute | solution.py:286
  54.2 10.5 %collective-permute-start.6 = (bf16[64,2048]{1,0:T(8,128)(2,1)S(1)}, bf16[64,2048]{1,0:T(8,128)(2,1)S(1)}, u32[]{:S(2)}, u32[]{:S(2)}) collective-permute-start(bf16[64,2048]{1,0:T(8,128)(2,1)S(1)} %get-tuple-element.33), channel_id=1, source_target_pairs={{1,0},{2,1},{3,2},{5,4},{6,5},{7,6},{9,8},{10,9},{11,10},{13,12},{... | collective-permute-start | bytes 786440 | tf_op jit(solution)/shard_map/ppermute | solution.py:286
  68.0 8.3 %collective-permute-start.7 = (bf16[64,2048]{1,0:T(8,128)(2,1)S(1)}, bf16[64,2048]{1,0:T(8,128)(2,1)S(1)}, u32[]{:S(2)}, u32[]{:S(2)}) collective-permute-start(bf16[64,2048]{1,0:T(8,128)(2,1)S(1)} %get-tuple-element.35), channel_id=1, source_target_pairs={{1,0},{2,1},{5,4},{6,5},{9,8},{10,9},{13,12},{14,13},{17,16},{18,1... | collective-permute-start | bytes 786440 | tf_op jit(solution)/shard_map/ppermute | solution.py:286
  79.4 10.5 %copy-start.2 = (bf16[1,300,2048]{2,1,0:T(8,128)(2,1)S(1)}, bf16[1,300,2048]{2,1,0:T(8,128)(2,1)}, u32[]{:S(2)}) copy-start(bf16[1,300,2048]{2,1,0:T(8,128)(2,1)} %param.7) | copy-start | bytes 3686404
  79.4 28.8 %copy-start.5 = (s32[1,64]{1,0:T(1,128)S(1)}, s32[1,64]{1,0:T(1,128)}, u32[]{:S(2)}) copy-start(s32[1,64]{1,0:T(1,128)} %offsets_ref.3) | copy-start | bytes 772
  79.5 8.8 %collective-permute-start.8 = (bf16[64,2048]{1,0:T(8,128)(2,1)S(1)}, bf16[64,2048]{1,0:T(8,128)(2,1)S(1)}, u32[]{:S(2)}, u32[]{:S(2)}) collective-permute-start(bf16[64,2048]{1,0:T(8,128)(2,1)S(1)} %get-tuple-element.37), channel_id=1, source_target_pairs={{1,0},{5,4},{9,8},{13,12},{17,16},{21,20},{25,24},{29,28}} | collective-permute-start | bytes 786440 | tf_op jit(solution)/shard_map/ppermute | solution.py:286
  89.9 52.8 %copy-start.3 = (s32[8,256]{1,0:T(8,128)S(1)}, s32[8,256]{1,0:T(8,128)}, u32[]{:S(2)}) copy-start(s32[8,256]{1,0:T(8,128)} %ids_ref.1) | copy-start | bytes 24580
  90.8 7.7 %collective-permute-start.9 = (bf16[256,300]{1,0:T(8,128)(2,1)S(1)}, bf16[256,300]{1,0:T(8,128)(2,1)S(1)}, u32[]{:S(2)}, u32[]{:S(2)}) collective-permute-start(bf16[256,300]{1,0:T(8,128)(2,1)S(1)} %get-tuple-element.40), channel_id=1, source_target_pairs={{0,1},{1,0},{2,3},{3,2},{4,5},{5,4},{6,7},{7,6},{8,9},{9,8},{10,11... | collective-permute-start | bytes 460808 | tf_op jit(solution)/shard_map/ppermute | solution.py:291
  98.6 8.9 %collective-permute-start.10 = (bf16[256,300]{1,0:T(8,128)(2,1)S(1)}, bf16[256,300]{1,0:T(8,128)(2,1)S(1)}, u32[]{:S(2)}, u32[]{:S(2)}) collective-permute-start(bf16[256,300]{1,0:T(8,128)(2,1)S(1)} %get-tuple-element.42), channel_id=1, source_target_pairs={{0,2},{1,3},{2,0},{3,1},{4,6},{5,7},{6,4},{7,5},{8,10},{9,11},{10,... | collective-permute-start | bytes 460808 | tf_op jit(solution)/shard_map/ppermute | solution.py:291
  110.2 3.9 %collective-permute-start.11 = (bf16[1,64,256]{2,1,0:T(8,128)(2,1)S(1)}, bf16[1,64,256]{2,1,0:T(8,128)(2,1)S(1)}, u32[]{:S(2)}, u32[]{:S(2)}) collective-permute-start(bf16[1,64,256]{2,1,0:T(8,128)(2,1)S(1)} %bitcast.11), channel_id=1, source_target_pairs={{0,1},{1,0},{2,3},{3,2},{4,5},{5,4},{6,7},{7,6},{8,9},{9,8},{10,11... | collective-permute-start | bytes 98312 | tf_op jit(solution)/shard_map/ppermute | solution.py:227
  114.1 5.4 %collective-permute-start.12 = (bf16[2,64,256]{2,1,0:T(8,128)(2,1)S(1)}, bf16[2,64,256]{2,1,0:T(8,128)(2,1)S(1)}, u32[]{:S(2)}, u32[]{:S(2)}) collective-permute-start(bf16[2,64,256]{2,1,0:T(8,128)(2,1)S(1)} %pad_maximum_fusion.3), channel_id=1, source_target_pairs={{0,2},{1,3},{2,0},{3,1},{4,6},{5,7},{6,4},{7,5},{8,10},{9,11},{10,... | collective-permute-start | bytes 196616 | tf_op jit(solution)/shard_map/ppermute | solution.py:227
  119.5 1.4 collective-permute-start.13
  120.9 8.4 %collective-permute-start.14 = (bf16[2,4,64,256]{3,2,1,0:T(8,128)(2,1)S(1)}, bf16[2,4,64,256]{3,2,1,0:T(8,128)(2,1)S(1)}, u32[]{:S(2)}, u32[]{:S(2)}) collective-permute-start(bf16[2,4,64,256]{3,2,1,0:T(8,128)(2,1)S(1)} %pad_maximum_fusion.2), channel_id=1, source_target_pairs={{0,8},{4,12},{8,0},{12,4},{16,24},{20,28},{24,16},{28,20},{1,9},{5... | collective-permute-start | bytes 786440 | tf_op jit(solution)/shard_map/ppermute | solution.py:227
  129.4 13.2 %collective-permute-start.15 = (bf16[4,4,64,256]{3,2,1,0:T(8,128)(2,1)S(1)}, bf16[4,4,64,256]{3,2,1,0:T(8,128)(2,1)S(1)}, u32[]{:S(2)}, u32[]{:S(2)}) collective-permute-start(bf16[4,4,64,256]{3,2,1,0:T(8,128)(2,1)S(1)} %pad_maximum_fusion.1), channel_id=1, source_target_pairs={{0,16},{4,20},{8,24},{12,28},{16,0},{20,4},{24,8},{28,12},{1,17},{... | collective-permute-start | bytes 1572872 | tf_op jit(solution)/shard_map/ppermute | solution.py:227
